TPU v7x, 512 devices: a whole 4x4x16 slice. The times are simulated.
512 devices in a mesh: dp: 64 (over x, z), ctx: 8 (over y, core).
Axes of the slice: x: 4, y: 4, z: 16, core: 2. Of those that a mesh axis runs over, the one named last changes fastest.
Arguments:
- projections: bfloat16 [131072, 6144], P(('dp', 'ctx')), may hold values from -6 to 6
- block_source: int32 [64, 8, 2], P('dp', 'ctx'), may hold values from 0 to 1023, as said below
- clip_ids: int32 [64, 16], P('dp'), may hold values from 0 to 8, as said below
- out_weight: bfloat16 [2048, 1536], P('dp'), may hold values from -1 to 1
Outputs:
- mixed: bfloat16 [131072, 1536], P(('dp', 'ctx'))
Inputs may be any that keep to these rules, and one draw needn't show every extreme that they name: `block_source`: arrival block a lies on the device numbered a // 2 in dp-major order (dp index a // (2 * 8), ctx index (a // 2) % 8). The block that fills pack block (o, j, l) lies on the device with the same ctx index j and dp index o or o XOR 1. Every arrival block fills exactly one pack block. `clip_ids`: in each pack the clip numbers start at 0, never fall and rise by at most one from block to block; every clip spans 1 to 8 blocks, and in every pack some clip spans exactly 8 blocks.
All inputs are finite; a program needn't handle non-finite values.
Results may differ from a plain program's by a relative error of at most 0.0057.
Values may be sent and summed in bfloat16 or wider, within the bound.
A program may use at most 64 MiB of HBM per device.

v0:
```python
import math
import jax
import jax.numpy as jnp
from jax import lax
from jax.sharding import PartitionSpec as P

HEAD = 128
big_negative = -1e30


def partner(value, axis, bit):
    mask = 2**bit
    pairs = [(source, source ^ mask) for source in range(lax.axis_size(axis))]
    return lax.ppermute(value, axis, pairs)


def soft_weights(scores, allowed):
    masked = jnp.where(allowed, scores, big_negative)
    row_max = jnp.max(masked, axis=-1, keepdims=True)
    exponent = jnp.exp(masked - row_max)
    return (exponent / jnp.sum(exponent, axis=-1, keepdims=True)).astype(jnp.bfloat16)


def attend_dense(queries, key_rows, value_rows, token_clip, scaling):
    token_count, head_count, head_size = queries.shape
    step_size = min(token_count, 512)
    step_count = token_count // step_size
    query_steps = queries.reshape(step_count, step_size, head_count, head_size)
    clip_steps = token_clip.reshape(step_count, step_size)

    def one_step(arguments):
        query_block, clip_block = arguments
        scores = (
            jnp.einsum("qhe,khe->hqk", query_block, key_rows, preferred_element_type=jnp.float32)
            * scaling
        )
        allowed = (clip_block[:, None] == token_clip[None, :])[None]
        weights = soft_weights(scores, allowed)
        return jnp.einsum(
            "hqk,khe->qhe", weights, value_rows, preferred_element_type=jnp.float32
        ).astype(jnp.bfloat16)

    outputs = lax.map(one_step, (query_steps, clip_steps))
    return outputs.reshape(token_count, head_count, head_size)


def body(projections, block_source, clip_ids, out_weight):
    ctx_count = lax.axis_size("ctx")
    local_rows, row_width = projections.shape
    local_blocks = block_source.shape[2]
    block_rows = local_rows // local_blocks
    own_blocks = projections.reshape(local_blocks, block_rows, row_width)
    partner_blocks = partner(own_blocks, "dp", 0)
    source_ids = block_source.reshape(local_blocks)
    from_partner = source_ids // (local_blocks * ctx_count) != lax.axis_index("dp")
    chosen_slot = source_ids % local_blocks + local_blocks * from_partner.astype(jnp.int32)
    candidates = jnp.concatenate([own_blocks, partner_blocks], axis=0)
    packed = jnp.take(candidates, chosen_slot, axis=0)
    local_heads = row_width // (3 * HEAD) // ctx_count
    grouped = packed.reshape(local_rows, ctx_count, local_heads, 3 * HEAD)
    block_clip = clip_ids.reshape(-1)
    token_clip = jnp.repeat(block_clip, block_rows)
    scaling = 1.0 / math.sqrt(HEAD)
    regrouped = lax.all_to_all(grouped, "ctx", split_axis=1, concat_axis=0, tiled=True)
    token_count = regrouped.shape[0]
    item_count = regrouped.shape[2]
    features = regrouped.reshape(token_count, item_count, 3 * HEAD)
    queries = features[:, :, :HEAD]
    key_rows = features[:, :, HEAD : 2 * HEAD]
    value_rows = features[:, :, 2 * HEAD :]
    attended = attend_dense(queries, key_rows, value_rows, token_clip, scaling)
    merged = attended.reshape(local_rows * ctx_count, local_heads * HEAD)
    attention_rows = lax.all_to_all(merged, "ctx", split_axis=0, concat_axis=1, tiled=True)
    result = jnp.dot(
        attention_rows,
        lax.all_gather(out_weight, "dp", axis=0, tiled=True),
        preferred_element_type=jnp.float32,
    )
    return result.astype(jnp.bfloat16)


def solution(mesh):
    return jax.shard_map(
        body,
        mesh=mesh,
        in_specs=(P(("dp", "ctx"), None), P("dp", "ctx", None), P("dp", None), P("dp", None)),
        out_specs=P(("dp", "ctx"), None),
        check_vma=False,
    )
```

profile of v0, /device:TPU:8, one launch (start us, length us, event | category | flops | bytes accessed | tf_op | source)
XLA Modules:
  0.0 276.1 jit_solution(7214846663131477792)
XLA Ops:
  6.5 3.8 %collective-permute-start = (bf16[2,128,6144]{2,1,0:T(8,128)(2,1)}, bf16[2,128,6144]{2,1,0:T(8,128)(2,1)S(1)}, u32[]{:S(2)}, u32[]{:S(2)}) collective-permute-start(bf16[2,128,6144]{2,1,0:T(8,128)(2,1)} %bitcast.87), channel_id=1, source_target_pairs={{0,8},{8,0},{16,24},{24,16},{32,40},{40,32},{48,56},{56,48},{64,72... | collective-permute-start | bytes 9437192 | tf_op jit(solution)/shard_map/ppermute | solution.py:14
  10.4 0.7 fusion.31
  11.0 0.7 compare_and_fusion
  11.7 0.1 broadcast_bitcast_fusion.2
  11.8 66.9 %collective-permute-done = bf16[2,128,6144]{2,1,0:T(8,128)(2,1)S(1)} collective-permute-done((bf16[2,128,6144]{2,1,0:T(8,128)(2,1)}, bf16[2,128,6144]{2,1,0:T(8,128)(2,1)S(1)}, u32[]{:S(2)}, u32[]{:S(2)}) %collective-permute-start) | collective-permute-done | bytes 3145760 | tf_op jit(solution)/shard_map/ppermute | solution.py:14
  78.7 5.1 %pad_maximum_fusion = bf16[4,128,6144]{2,1,0:T(8,128)(2,1)} fusion(bf16[2,128,6144]{2,1,0:T(8,128)(2,1)S(1)} %collective-permute-done, bf16[2,128,6144]{2,1,0:T(8,128)(2,1)} %bitcast.88), kind=kLoop, calls=%fused_computation.27 | loop fusion | flops 3145728 | bytes 12582912 | tf_op jit(solution)/shard_map/concatenate | solution.py:57
  83.7 3.5 %gather_fusion = bf16[2,128,6144]{2,1,0:T(8,128)(2,1)S(1)} fusion(bf16[4,128,6144]{2,1,0:T(8,128)(2,1)} %pad_maximum_fusion, s32[1024]{0:T(1024)S(1)} %pad_clamp_fusion), kind=kCustom, calls=%fused_computation | custom fusion | bytes 6291464 | tf_op jit(solution)/shard_map/jit(_take)/gather | solution.py:58
  87.3 3.5 %gather.7 = bf16[256,8,2,384]{3,2,1,0:T(2,128)(2,1)} reshape(bf16[2,128,6144]{2,1,0:T(8,128)(2,1)S(1)} %gather_fusion) | data formatting | bytes 6291456 | tf_op jit(solution)/shard_map/jit(_take)/gather | solution.py:58
  90.8 5.0 %broadcast_select_fusion = bf16[256,8,2,384]{3,2,1,0:T(2,128)(2,1)S(1)} fusion(bf16[256,8,2,384]{3,2,1,0:T(2,128)(2,1)} %gather.7, pred[256]{0:T(512)(128)(4,1)S(1)} %broadcast_bitcast_fusion.2), kind=kLoop, calls=%fused_computation.28 | loop fusion | flops 1572864 | bytes 6291712 | tf_op jit(solution)/shard_map/jit(_take)/select_n | solution.py:58
  95.8 4.1 %copy.12 = bf16[256,8,2,384]{3,2,0,1:T(2,128)(2,1)} copy(bf16[256,8,2,384]{3,2,1,0:T(2,128)(2,1)S(1)} %broadcast_select_fusion) | data formatting | bytes 6291456 | tf_op jit(solution)/shard_map/jit(_take)/select_n | solution.py:58
  99.9 5.0 %all-to-all-start = ((bf16[256,8,2,384]{3,2,0,1:T(2,128)(2,1)}), bf16[256,8,2,384]{3,2,0,1:T(2,128)(2,1)S(1)}, u32[]{:S(2)}, u32[]{:S(2)}) async-start(bf16[256,8,2,384]{3,2,0,1:T(2,128)(2,1)} %copy.12), calls=%async_computation | async-start | bytes 6291456 | tf_op jit(solution)/shard_map/all_to_all | solution.py:64
  104.9 0.0 all-gather.2.cloned.1.call-start
  104.9 0.7 all-gather.2.cloned.1.call-update
  105.6 0.5 broadcast.219
  106.1 0.0 copy-done.1
  106.1 0.6 reduce.3
  106.7 0.1 broadcast_in_dim.47
  106.8 0.1 broadcast_bitcast_fusion.1
  106.9 35.0 %all-to-all-done = bf16[256,8,2,384]{3,2,0,1:T(2,128)(2,1)S(1)} async-done(((bf16[256,8,2,384]{3,2,0,1:T(2,128)(2,1)}), bf16[256,8,2,384]{3,2,0,1:T(2,128)(2,1)S(1)}, u32[]{:S(2)}, u32[]{:S(2)}) %all-to-all-start) | async-done | bytes 3145760 | tf_op jit(solution)/shard_map/all_to_all | solution.py:64
  141.9 0.6 copy.13
  142.4 0.0 copy-start
  142.5 1.9 fusion.37
  144.3 53.7 %while.11 = (s32[]{:T(128)}, bf16[4,512,2,128]{3,2,1,0:T(2,128)(2,1)S(1)}, s32[4,512]{1,0:T(4,128)S(1)}, bf16[4,512,2,128]{3,1,0,2:T(8,128)(2,1)}, bf16[2048,2,1...) while((s32[]{:T(128)}, ...), condition=%wide.region_3.4_spmd.clone, body=%wide.region_0.3_spmd.clone.sunk | while | flops 1087506432 | bytes 22051484 | solution.py:43
  144.3 0.1 broadcast_bitcast_fusion.4
  144.4 0.7 broadcast_compare_fusion.2
  145.1 7.7 %fusion.51 = (f32[2,512]{1,0:T(2,128)S(1)}, f32[2,512,2048]{2,1,0:T(8,128)}) fusion(pred[512,2048]{1,0:T(8,128)(4,1)S(1)} %broadcast_compare_fusion.2, bf16[2048,2,128]{2,0,1:T(8,128)(2,1)} %get-tuple-element.167, bf16[4,512,2,128]{3,1,0,2:T(8,128)(2,1)} %get-tuple-element.166, s32[]{:T(128)} %get-tuple-element.155), kind=kOutput, calls=%fused_computation.56.clone.1 | convolution fusion | flops 545261568 | bytes 10752512 | tf_op jit(solution)/shard_map/while/body/eval_jaxpr/sub | solution.py:20
  152.7 4.7 %fusion.52 = bf16[1,512,2,128]{3,1,2,0:T(8,128)(2,1)S(1)} fusion(bf16[2048,2,128]{2,0,1:T(8,128)(2,1)S(1)} %get-tuple-element.168, f32[2,512,2048]{2,1,0:T(8,128)} %get-tuple-element.145, f32[2,512]{1,0:T(2,128)S(1)} %get-tuple-element.146), kind=kOutput, calls=%fused_computation.13.clone.1 | convolution fusion | flops 541196288 | bytes 9703424 | tf_op jit(solution)/shard_map/while/body/eval_jaxpr/hqk,khe->qhe/dot_general | solution.py:39
  157.4 0.3 copy_dynamic-update-slice_fusion.2
  157.8 0.1 broadcast_bitcast_fusion.4
  157.8 0.7 broadcast_compare_fusion.2
  158.5 7.7 %fusion.51 = (f32[2,512]{1,0:T(2,128)S(1)}, f32[2,512,2048]{2,1,0:T(8,128)}) fusion(pred[512,2048]{1,0:T(8,128)(4,1)S(1)} %broadcast_compare_fusion.2, bf16[2048,2,128]{2,0,1:T(8,128)(2,1)} %get-tuple-element.167, bf16[4,512,2,128]{3,1,0,2:T(8,128)(2,1)} %get-tuple-element.166, s32[]{:T(128)} %get-tuple-element.155), kind=kOutput, calls=%fused_computation.56.clone.1 | convolution fusion | flops 545261568 | bytes 10752512 | tf_op jit(solution)/shard_map/while/body/eval_jaxpr/sub | solution.py:20
  166.2 4.7 %fusion.52 = bf16[1,512,2,128]{3,1,2,0:T(8,128)(2,1)S(1)} fusion(bf16[2048,2,128]{2,0,1:T(8,128)(2,1)S(1)} %get-tuple-element.168, f32[2,512,2048]{2,1,0:T(8,128)} %get-tuple-element.145, f32[2,512]{1,0:T(2,128)S(1)} %get-tuple-element.146), kind=kOutput, calls=%fused_computation.13.clone.1 | convolution fusion | flops 541196288 | bytes 9703424 | tf_op jit(solution)/shard_map/while/body/eval_jaxpr/hqk,khe->qhe/dot_general | solution.py:39
  170.9 0.3 copy_dynamic-update-slice_fusion.2
  171.2 0.1 broadcast_bitcast_fusion.4
  171.3 0.7 broadcast_compare_fusion.2
  171.9 7.7 %fusion.51 = (f32[2,512]{1,0:T(2,128)S(1)}, f32[2,512,2048]{2,1,0:T(8,128)}) fusion(pred[512,2048]{1,0:T(8,128)(4,1)S(1)} %broadcast_compare_fusion.2, bf16[2048,2,128]{2,0,1:T(8,128)(2,1)} %get-tuple-element.167, bf16[4,512,2,128]{3,1,0,2:T(8,128)(2,1)} %get-tuple-element.166, s32[]{:T(128)} %get-tuple-element.155), kind=kOutput, calls=%fused_computation.56.clone.1 | convolution fusion | flops 545261568 | bytes 10752512 | tf_op jit(solution)/shard_map/while/body/eval_jaxpr/sub | solution.py:20
  179.6 4.7 %fusion.52 = bf16[1,512,2,128]{3,1,2,0:T(8,128)(2,1)S(1)} fusion(bf16[2048,2,128]{2,0,1:T(8,128)(2,1)S(1)} %get-tuple-element.168, f32[2,512,2048]{2,1,0:T(8,128)} %get-tuple-element.145, f32[2,512]{1,0:T(2,128)S(1)} %get-tuple-element.146), kind=kOutput, calls=%fused_computation.13.clone.1 | convolution fusion | flops 541196288 | bytes 9703424 | tf_op jit(solution)/shard_map/while/body/eval_jaxpr/hqk,khe->qhe/dot_general | solution.py:39
  184.3 0.3 copy_dynamic-update-slice_fusion.2
  184.6 0.1 broadcast_bitcast_fusion.4
  184.7 0.7 broadcast_compare_fusion.2
  185.3 7.7 %fusion.51 = (f32[2,512]{1,0:T(2,128)S(1)}, f32[2,512,2048]{2,1,0:T(8,128)}) fusion(pred[512,2048]{1,0:T(8,128)(4,1)S(1)} %broadcast_compare_fusion.2, bf16[2048,2,128]{2,0,1:T(8,128)(2,1)} %get-tuple-element.167, bf16[4,512,2,128]{3,1,0,2:T(8,128)(2,1)} %get-tuple-element.166, s32[]{:T(128)} %get-tuple-element.155), kind=kOutput, calls=%fused_computation.56.clone.1 | convolution fusion | flops 545261568 | bytes 10752512 | tf_op jit(solution)/shard_map/while/body/eval_jaxpr/sub | solution.py:20
  193.0 4.7 %fusion.52 = bf16[1,512,2,128]{3,1,2,0:T(8,128)(2,1)S(1)} fusion(bf16[2048,2,128]{2,0,1:T(8,128)(2,1)S(1)} %get-tuple-element.168, f32[2,512,2048]{2,1,0:T(8,128)} %get-tuple-element.145, f32[2,512]{1,0:T(2,128)S(1)} %get-tuple-element.146), kind=kOutput, calls=%fused_computation.13.clone.1 | convolution fusion | flops 541196288 | bytes 9703424 | tf_op jit(solution)/shard_map/while/body/eval_jaxpr/hqk,khe->qhe/dot_general | solution.py:39
  197.7 0.3 copy_dynamic-update-slice_fusion.2
  198.0 0.7 all_to_all.28
  198.7 18.5 %all_to_all.34 = bf16[8,256,256]{2,1,0:T(8,128)(2,1)S(1)} all-to-all(bf16[8,256,256]{2,1,0:T(8,128)(2,1)S(1)} %all_to_all.28), channel_id=1, replica_groups=mesh['dp'=64,'ctx'=8] {'ctx'}, dimensions={0} | all-to-all | bytes 2097152 | tf_op jit(solution)/shard_map/all_to_all | solution.py:73
  217.2 0.5 copy.16
  217.7 46.0 %all-gather.2.cloned.1.call-done = bf16[2048,1536]{1,0:T(8,128)(2,1)} async-done(((bf16[32,1536]{1,0:T(8,128)(2,1)}), bf16[2048,1536]{1,0:T(8,128)(2,1)}) %all-gather.2.cloned.1.call-update) | async-done | bytes 6291472 | tf_op jit(solution)/shard_map/all_gather | solution.py:76
  263.7 5.5 %convolution_convert_fusion = bf16[256,1536]{1,0:T(8,128)(2,1)} fusion(bf16[256,2048]{0,1:T(8,128)(2,1)S(1)} %bitcast.85, bf16[2048,1536]{1,0:T(8,128)(2,1)} %all-gather.2.cloned.1.call-done), kind=kOutput, calls=%fused_computation.29 | convolution fusion | flops 1611005952 | bytes 8126464 | tf_op jit(solution)/shard_map/dot_general | solution.py:74
  (9 shorter events, 0.0 us)
Async XLA Ops:
  6.5 72.1 %collective-permute-start = (bf16[2,128,6144]{2,1,0:T(8,128)(2,1)}, bf16[2,128,6144]{2,1,0:T(8,128)(2,1)S(1)}, u32[]{:S(2)}, u32[]{:S(2)}) collective-permute-start(bf16[2,128,6144]{2,1,0:T(8,128)(2,1)} %bitcast.87), channel_id=1, source_target_pairs={{0,8},{8,0},{16,24},{24,16},{32,40},{40,32},{48,56},{56,48},{64,72... | collective-permute-start | bytes 9437192 | tf_op jit(solution)/shard_map/ppermute | solution.py:14
  99.9 6.3 %copy-start.1 = (s32[1,16]{1,0:T(1,128)S(1)}, s32[1,16]{1,0:T(1,128)}, u32[]{:S(2)}) copy-start(s32[1,16]{1,0:T(1,128)} %param.8) | copy-start | bytes 196
  99.9 42.0 %all-to-all-start = ((bf16[256,8,2,384]{3,2,0,1:T(2,128)(2,1)}), bf16[256,8,2,384]{3,2,0,1:T(2,128)(2,1)S(1)}, u32[]{:S(2)}, u32[]{:S(2)}) async-start(bf16[256,8,2,384]{3,2,0,1:T(2,128)(2,1)} %copy.12), calls=%async_computation | async-start | bytes 6291456 | tf_op jit(solution)/shard_map/all_to_all | solution.py:64
  104.9 158.8 %all-gather.2.cloned.1.call-start = ((), (), s32[]{:S(2)}) async-start(), calls=%async_computation.2 | async-start | bytes 6389760 | tf_op jit(solution)/shard_map/all_gather | solution.py:76
  142.4 1.9 copy-start
Sparse Core Ops, SparseCore 0:
  108.7 155.0 all-gather.1
where the time goes:
time: 277 us; the launch traced here: 276 us
  waiting for transfers between devices  149 us (54%)
  matrix products  54.9 us (20%)
  blocking collectives  18.5 us (7%)
  local copies, waits for them, and re-layouts  17.1 us (6%)
  other arithmetic  14.6 us (5%)
  between operations  13.5 us (5%)
  starting transfers between devices  8.87 us (3%)
    ppermute x1, waiting for transfers between devices, partner(): return lax.ppermute(value, axis, pairs)  66.9 us
    all_gather x1, waiting for transfers between devices, body(): lax.all_gather(out_weight, 'dp', axis=0, tiled=True)  46 us
    all_to_all x1, waiting for transfers between devices, body(): lax.all_to_all(grouped, 'ctx', split_axis=1, concat_axis=0, tiled=True)  35 us
    sub x4, matrix products, soft_weights(): exponent = jnp.exp(masked - row_max)  30.7 us
    dot_general x4, matrix products, one_step(): jnp.einsum('hqk,khe->qhe', weights, value_rows, preferred_element_type=jn...  18.7 us
    all_to_all x1, blocking collectives, body(): lax.all_to_all(merged, 'ctx', split_axis=0, concat_axis=1, tiled=True)  18.5 us
    gather x2, local copies, waits for them, and re-layouts, body(): packed = jnp.take(candidates, chosen_slot, axis=0)  7.07 us
    select_n x2, other arithmetic, body(): packed = jnp.take(candidates, chosen_slot, axis=0)  5.63 us
  transfers between devices with their start and end apart: 3, of which 3 were waited for; matrix products, arithmetic and copies ran while one was open for 21% of the time, Pallas kernels for 0%

commit v1 on v0

--- a/solution.py
+++ b/solution.py
@@ -61,7 +61,10 @@
     block_clip = clip_ids.reshape(-1)
     token_clip = jnp.repeat(block_clip, block_rows)
     scaling = 1.0 / math.sqrt(HEAD)
-    regrouped = lax.all_to_all(grouped, "ctx", split_axis=1, concat_axis=0, tiled=True)
+    regrouped = jnp.concatenate(
+        lax.all_to_all(jnp.stack(jnp.split(grouped, lax.axis_size("ctx"), axis=1)), "ctx", 0, 0),
+        axis=0,
+    )
     token_count = regrouped.shape[0]
     item_count = regrouped.shape[2]
     features = regrouped.reshape(token_count, item_count, 3 * HEAD)

time: 277 us -> 280 us (1.011)
  the two profiles are of different devices: /device:TPU:8 before, /device:TPU:16 now
where the time goes in v1:
time: 280 us
  waiting for transfers between devices  153 us (55%)
  matrix products  45.5 us (16%)
  local copies, waits for them, and re-layouts  26.2 us (9%)
  blocking collectives  18.5 us (7%)
  other arithmetic  14.7 us (5%)
  between operations  13.5 us (5%)
  starting transfers between devices  8.75 us (3%)
    ppermute x1, waiting for transfers between devices, partner(): return lax.ppermute(value, axis, pairs)  66.9 us
    all_gather x1, waiting for transfers between devices, body(): lax.all_gather(out_weight, 'dp', axis=0, tiled=True)  52.2 us
    all_to_all x1, waiting for transfers between devices, body(): lax.all_to_all(jnp.stack(jnp.split(grouped, lax.axis_size('ctx'), axis=1)...  33.1 us
    sub x4, matrix products, soft_weights(): exponent = jnp.exp(masked - row_max)  20.3 us
    dot_general x4, matrix products, one_step(): jnp.einsum('hqk,khe->qhe', weights, value_rows, preferred_element_type=jn...  19.7 us
    all_to_all x1, blocking collectives, body(): lax.all_to_all(merged, 'ctx', split_axis=0, concat_axis=1, tiled=True)  18.5 us
    unnamed x15, local copies, waits for them, and re-layouts  9.22 us
    gather x2, local copies, waits for them, and re-layouts, body(): packed = jnp.take(candidates, chosen_slot, axis=0)  7.06 us
  transfers between devices with their start and end apart: 3, of which 3 were waited for; matrix products, arithmetic and copies ran while one was open for 19% of the time, Pallas kernels for 0%

profile of v1, /device:TPU:16, one launch (start us, length us, event | category | flops | bytes accessed | tf_op | source)
XLA Modules:
  0.0 280.0 jit_solution(17478217401842957548)
XLA Ops:
  6.5 3.8 %collective-permute-start = (bf16[2,128,6144]{2,1,0:T(8,128)(2,1)}, bf16[2,128,6144]{2,1,0:T(8,128)(2,1)S(1)}, u32[]{:S(2)}, u32[]{:S(2)}) collective-permute-start(bf16[2,128,6144]{2,1,0:T(8,128)(2,1)} %bitcast.129), channel_id=1, source_target_pairs={{0,8},{8,0},{16,24},{24,16},{32,40},{40,32},{48,56},{56,48},{64,72... | collective-permute-start | bytes 9437192 | tf_op jit(solution)/shard_map/ppermute | solution.py:14
  10.4 0.7 fusion.39
  11.0 0.7 compare_and_fusion
  11.8 66.9 %collective-permute-done = bf16[2,128,6144]{2,1,0:T(8,128)(2,1)S(1)} collective-permute-done((bf16[2,128,6144]{2,1,0:T(8,128)(2,1)}, bf16[2,128,6144]{2,1,0:T(8,128)(2,1)S(1)}, u32[]{:S(2)}, u32[]{:S(2)}) %collective-permute-start) | collective-permute-done | bytes 3145760 | tf_op jit(solution)/shard_map/ppermute | solution.py:14
  78.7 5.1 %pad_maximum_fusion = bf16[4,128,6144]{2,1,0:T(8,128)(2,1)} fusion(bf16[2,128,6144]{2,1,0:T(8,128)(2,1)S(1)} %collective-permute-done, bf16[2,128,6144]{2,1,0:T(8,128)(2,1)} %bitcast.130), kind=kLoop, calls=%fused_computation.27 | loop fusion | flops 3145728 | bytes 12582912 | tf_op jit(solution)/shard_map/concatenate | solution.py:57
  83.7 3.5 %gather_fusion = bf16[2,128,6144]{2,1,0:T(8,128)(2,1)S(1)} fusion(bf16[4,128,6144]{2,1,0:T(8,128)(2,1)} %pad_maximum_fusion, s32[1024]{0:T(1024)S(1)} %pad_clamp_fusion), kind=kCustom, calls=%fused_computation | custom fusion | bytes 6291464 | tf_op jit(solution)/shard_map/jit(_take)/gather | solution.py:58
  87.3 3.5 %gather.7 = bf16[256,8,2,384]{3,2,1,0:T(2,128)(2,1)} reshape(bf16[2,128,6144]{2,1,0:T(8,128)(2,1)S(1)} %gather_fusion) | data formatting | bytes 6291456 | tf_op jit(solution)/shard_map/jit(_take)/gather | solution.py:58
  90.8 5.0 %broadcast_select_fusion = bf16[256,8,2,384]{3,2,1,0:T(2,128)(2,1)S(1)} fusion(bf16[256,8,2,384]{3,2,1,0:T(2,128)(2,1)} %gather.7, pred[256]{0:T(512)(128)(4,1)S(1)} %broadcast_bitcast_fusion.2), kind=kLoop, calls=%fused_computation.28 | loop fusion | flops 1572864 | bytes 6291712 | tf_op jit(solution)/shard_map/jit(_take)/select_n | solution.py:58
  95.8 1.0 fusion.36
  96.8 1.0 fusion.35
  97.8 1.0 fusion.34
  98.8 1.0 fusion.33
  99.8 1.0 fusion.32
  100.9 1.1 fusion.31
  101.9 1.0 fusion.30
  102.9 1.0 fusion.29
  104.0 4.9 %all-to-all-start = ((bf16[8,256,1,2,384]{4,3,1,2,0:T(2,128)(2,1)}), bf16[8,256,1,2,384]{4,3,1,2,0:T(2,128)(2,1)S(1)}, u32[]{:S(2)}, u32[]{:S(2)}) async-start(bf16[8,256,1,2,384]{4,3,1,2,0:T(2,128)(2,1)} %fusion.29), calls=%async_computation | async-start | bytes 6291456 | tf_op jit(solution)/shard_map/all_to_all | solution.py:65
  108.9 0.7 all-gather.2.cloned.1.call-update
  109.6 0.6 broadcast.219
  110.2 0.7 reduce.3
  110.9 0.1 broadcast_in_dim.47
  111.1 33.1 %all-to-all-done = bf16[8,256,1,2,384]{4,3,1,2,0:T(2,128)(2,1)S(1)} async-done(((bf16[8,256,1,2,384]{4,3,1,2,0:T(2,128)(2,1)}), bf16[8,256,1,2,384]{4,3,1,2,0:T(2,128)(2,1)S(1)}, u32[]{:S(2)}, u32[]{:S(2)}) %all-to-all-start) | async-done | bytes 3145760 | tf_op jit(solution)/shard_map/all_to_all | solution.py:65
  144.2 2.2 fusion.45
  146.4 0.1 copy.35
  146.5 0.1 copy.36
  146.6 1.1 copy.37
  147.8 46.9 %while.11 = (s32[]{:T(128)}, bf16[4,512,2,128]{3,2,1,0:T(2,128)(2,1)}, s32[4,512]{1,0:T(4,128)S(1)}, bf16[4,512,2,128]{3,1,0,2:T(8,128)(2,1)S(1)}, bf16[2048,2,1...) while((s32[]{:T(128)}, ...), condition=%wide.region_3.4_spmd.clone, body=%wide.region_0.3_spmd.clone.sunk | while | flops 1087506432 | bytes 22051484 | solution.py:43
  147.8 0.7 broadcast_compare_fusion.2
  148.5 5.1 %fusion.59 = (f32[2,512]{1,0:T(2,128)S(1)}, f32[2,512,2048]{2,1,0:T(8,128)}) fusion(pred[512,2048]{1,0:T(8,128)(4,1)S(1)} %broadcast_compare_fusion.2, bf16[2048,2,128]{2,0,1:T(8,128)(2,1)S(1)} %get-tuple-element.153, bf16[4,512,2,128]{3,1,0,2:T(8,128)(2,1)S(1)} %get-tuple-element.152, s32[]{:T(128)} %get-tuple-element.141), kind=kOutput, calls=%fused_computation.72.clone.1 | convolution fusion | flops 545261568 | bytes 10752004 | tf_op jit(solution)/shard_map/while/body/eval_jaxpr/sub | solution.py:20
  153.6 4.9 %fusion.60 = bf16[1,512,2,128]{3,1,2,0:T(8,128)(2,1)S(1)} fusion(bf16[2048,2,128]{2,0,1:T(8,128)(2,1)} %get-tuple-element.154, f32[2,512,2048]{2,1,0:T(8,128)} %get-tuple-element.131, f32[2,512]{1,0:T(2,128)S(1)} %get-tuple-element.132), kind=kOutput, calls=%fused_computation.13.clone.1 | convolution fusion | flops 541196288 | bytes 9703424 | tf_op jit(solution)/shard_map/while/body/eval_jaxpr/hqk,khe->qhe/dot_general | solution.py:39
  158.5 1.0 copy_dynamic-update-slice_fusion.2
  159.6 0.7 broadcast_compare_fusion.2
  160.3 5.1 %fusion.59 = (f32[2,512]{1,0:T(2,128)S(1)}, f32[2,512,2048]{2,1,0:T(8,128)}) fusion(pred[512,2048]{1,0:T(8,128)(4,1)S(1)} %broadcast_compare_fusion.2, bf16[2048,2,128]{2,0,1:T(8,128)(2,1)S(1)} %get-tuple-element.153, bf16[4,512,2,128]{3,1,0,2:T(8,128)(2,1)S(1)} %get-tuple-element.152, s32[]{:T(128)} %get-tuple-element.141), kind=kOutput, calls=%fused_computation.72.clone.1 | convolution fusion | flops 545261568 | bytes 10752004 | tf_op jit(solution)/shard_map/while/body/eval_jaxpr/sub | solution.py:20
  165.3 4.9 %fusion.60 = bf16[1,512,2,128]{3,1,2,0:T(8,128)(2,1)S(1)} fusion(bf16[2048,2,128]{2,0,1:T(8,128)(2,1)} %get-tuple-element.154, f32[2,512,2048]{2,1,0:T(8,128)} %get-tuple-element.131, f32[2,512]{1,0:T(2,128)S(1)} %get-tuple-element.132), kind=kOutput, calls=%fused_computation.13.clone.1 | convolution fusion | flops 541196288 | bytes 9703424 | tf_op jit(solution)/shard_map/while/body/eval_jaxpr/hqk,khe->qhe/dot_general | solution.py:39
  170.3 1.0 copy_dynamic-update-slice_fusion.2
  171.3 0.7 broadcast_compare_fusion.2
  172.0 5.1 %fusion.59 = (f32[2,512]{1,0:T(2,128)S(1)}, f32[2,512,2048]{2,1,0:T(8,128)}) fusion(pred[512,2048]{1,0:T(8,128)(4,1)S(1)} %broadcast_compare_fusion.2, bf16[2048,2,128]{2,0,1:T(8,128)(2,1)S(1)} %get-tuple-element.153, bf16[4,512,2,128]{3,1,0,2:T(8,128)(2,1)S(1)} %get-tuple-element.152, s32[]{:T(128)} %get-tuple-element.141), kind=kOutput, calls=%fused_computation.72.clone.1 | convolution fusion | flops 545261568 | bytes 10752004 | tf_op jit(solution)/shard_map/while/body/eval_jaxpr/sub | solution.py:20
  177.0 4.9 %fusion.60 = bf16[1,512,2,128]{3,1,2,0:T(8,128)(2,1)S(1)} fusion(bf16[2048,2,128]{2,0,1:T(8,128)(2,1)} %get-tuple-element.154, f32[2,512,2048]{2,1,0:T(8,128)} %get-tuple-element.131, f32[2,512]{1,0:T(2,128)S(1)} %get-tuple-element.132), kind=kOutput, calls=%fused_computation.13.clone.1 | convolution fusion | flops 541196288 | bytes 9703424 | tf_op jit(solution)/shard_map/while/body/eval_jaxpr/hqk,khe->qhe/dot_general | solution.py:39
  182.0 1.0 copy_dynamic-update-slice_fusion.2
  183.0 0.7 broadcast_compare_fusion.2
  183.7 5.1 %fusion.59 = (f32[2,512]{1,0:T(2,128)S(1)}, f32[2,512,2048]{2,1,0:T(8,128)}) fusion(pred[512,2048]{1,0:T(8,128)(4,1)S(1)} %broadcast_compare_fusion.2, bf16[2048,2,128]{2,0,1:T(8,128)(2,1)S(1)} %get-tuple-element.153, bf16[4,512,2,128]{3,1,0,2:T(8,128)(2,1)S(1)} %get-tuple-element.152, s32[]{:T(128)} %get-tuple-element.141), kind=kOutput, calls=%fused_computation.72.clone.1 | convolution fusion | flops 545261568 | bytes 10752004 | tf_op jit(solution)/shard_map/while/body/eval_jaxpr/sub | solution.py:20
  188.8 4.9 %fusion.60 = bf16[1,512,2,128]{3,1,2,0:T(8,128)(2,1)S(1)} fusion(bf16[2048,2,128]{2,0,1:T(8,128)(2,1)} %get-tuple-element.154, f32[2,512,2048]{2,1,0:T(8,128)} %get-tuple-element.131, f32[2,512]{1,0:T(2,128)S(1)} %get-tuple-element.132), kind=kOutput, calls=%fused_computation.13.clone.1 | convolution fusion | flops 541196288 | bytes 9703424 | tf_op jit(solution)/shard_map/while/body/eval_jaxpr/hqk,khe->qhe/dot_general | solution.py:39
  193.7 1.0 copy_dynamic-update-slice_fusion.2
  194.7 1.7 all_to_all.18
  196.4 18.5 %all_to_all.24 = bf16[8,256,256]{2,1,0:T(8,128)(2,1)S(1)} all-to-all(bf16[8,256,256]{2,1,0:T(8,128)(2,1)S(1)} %all_to_all.18), channel_id=1, replica_groups=mesh['dp'=64,'ctx'=8] {'ctx'}, dimensions={0} | all-to-all | bytes 2097152 | tf_op jit(solution)/shard_map/all_to_all | solution.py:76
  214.9 0.5 copy.24
  215.4 52.2 %all-gather.2.cloned.1.call-done = bf16[2048,1536]{1,0:T(8,128)(2,1)} async-done(((bf16[32,1536]{1,0:T(8,128)(2,1)}), bf16[2048,1536]{1,0:T(8,128)(2,1)}) %all-gather.2.cloned.1.call-update) | async-done | bytes 6291472 | tf_op jit(solution)/shard_map/all_gather | solution.py:79
  267.7 5.5 %convolution_convert_fusion = bf16[256,1536]{1,0:T(8,128)(2,1)} fusion(bf16[256,2048]{0,1:T(8,128)(2,1)S(1)} %bitcast.127, bf16[2048,1536]{1,0:T(8,128)(2,1)} %all-gather.2.cloned.1.call-done), kind=kOutput, calls=%fused_computation.29 | convolution fusion | flops 1611005952 | bytes 8126464 | tf_op jit(solution)/shard_map/dot_general | solution.py:77
  (16 shorter events, 0.5 us)
Async XLA Ops:
  6.5 72.1 %collective-permute-start = (bf16[2,128,6144]{2,1,0:T(8,128)(2,1)}, bf16[2,128,6144]{2,1,0:T(8,128)(2,1)S(1)}, u32[]{:S(2)}, u32[]{:S(2)}) collective-permute-start(bf16[2,128,6144]{2,1,0:T(8,128)(2,1)} %bitcast.129), channel_id=1, source_target_pairs={{0,8},{8,0},{16,24},{24,16},{32,40},{40,32},{48,56},{56,48},{64,72... | collective-permute-start | bytes 9437192 | tf_op jit(solution)/shard_map/ppermute | solution.py:14
  104.0 6.3 %copy-start = (s32[1,16]{1,0:T(1,128)S(1)}, s32[1,16]{1,0:T(1,128)}, u32[]{:S(2)}) copy-start(s32[1,16]{1,0:T(1,128)} %param.8) | copy-start | bytes 196
  104.0 40.2 %all-to-all-start = ((bf16[8,256,1,2,384]{4,3,1,2,0:T(2,128)(2,1)}), bf16[8,256,1,2,384]{4,3,1,2,0:T(2,128)(2,1)S(1)}, u32[]{:S(2)}, u32[]{:S(2)}) async-start(bf16[8,256,1,2,384]{4,3,1,2,0:T(2,128)(2,1)} %fusion.29), calls=%async_computation | async-start | bytes 6291456 | tf_op jit(solution)/shard_map/all_to_all | solution.py:65
  108.9 158.8 %all-gather.2.cloned.1.call-start = ((), (), s32[]{:S(2)}) async-start(), calls=%async_computation.2 | async-start | bytes 6389760 | tf_op jit(solution)/shard_map/all_gather | solution.py:79
Sparse Core Ops, SparseCore 0:
  112.6 154.9 all-gather.1
